TPU v7x, 512 devices: a whole 4x4x16 slice. The times are simulated.
512 devices in a mesh: domain: 64 (over x, y, z_lo), member: 8 (over z_hi, core).
Axes of the slice: x: 4, y: 4, z: 16 (z_hi: 4, z_lo: 4; z = z_hi * 4 + z_lo), core: 2. Of those that a mesh axis runs over, the one named last changes fastest.
Arguments:
- inputs: bfloat16 [16, 12288, 1024], P('member', 'domain')
- norm_gain: bfloat16 [1024], P('member'), may hold values from 0.099609375 to 1.8984375
- w_query: bfloat16 [1024, 512], P('member')
- w_key: bfloat16 [1024, 512], P('member')
- w_value: bfloat16 [1024, 512], P('member'), may hold values from -0.1875 to 0.1875
- w_out: bfloat16 [512, 1024], P('member'), may hold values from -0.75 to 0.75
- neighbors: int32 [192, 9], P('domain'), may hold values from 0 to 191, as said below
- slot_valid: int32 [192, 9], P('domain'), may hold values from 0 to 1, as said below
- output_cotangent: bfloat16 [16, 12288, 1024], P('member', 'domain'), may hold values from -1.5 to 1.5
Outputs:
- attn_out: bfloat16 [16, 12288, 1024], P('member', 'domain')
- d_input: bfloat16 [16, 12288, 1024], P('member', 'domain')
- grad_wout: float32 [512, 1024], P('member')
Inputs may be any that keep to these rules, and one draw needn't show every extreme that they name: `neighbors`: slot 0 of block b names b. The blocks named by the valid slots of b are distinct and lie within blocks (b // 3 - 1) * 3 to (b // 3 + 2) * 3 - 1. An invalid slot names b. `slot_valid`: slot 0 is always 1.
All inputs are finite; a program needn't handle non-finite values.
Results may differ from a plain program's by a relative error of at most 0.019.
Values may be sent and summed in bfloat16 or wider, within the bound.
No kernel may reach another device: no remote copies, remote signals or barrier semaphores. Data moves between devices by JAX's collectives and lax.ppermute only.
A program may use at most 128 MiB of HBM per device.

v0:
```python
import jax
import jax.numpy as jnp
from jax import lax
from jax.sharding import PartitionSpec as P

HEAD_DIM = 64
EPSILON = 1e-06
MASKED = -1e30


def extended_2(value, sides, width):
    for axis, dim in sides:
        peers, length = (lax.axis_size(axis), value.shape[dim])
        up = [(i, (i + 1) % peers) for i in range(peers - 1)]
        down = [(j, i) for i, j in up]
        last = lax.slice_in_dim(value, length - width, length, axis=dim)
        initial = lax.slice_in_dim(value, 0, width, axis=dim)
        before = lax.ppermute(last, axis, up)
        after = lax.ppermute(initial, axis, down)
        value = jnp.concatenate([before, value, after], axis=dim)
    return value


def pair_columns(field, pair_index, pair_width):
    return lax.dynamic_slice_in_dim(field, pair_index * pair_width, pair_width, field.ndim - 1)


def shards(
    inputs, norm_gain, w_query, w_key, w_value, w_out, neighbors, slot_valid, output_cotangent
):
    samples, length, model_width = inputs.shape
    block_count, slot_count = neighbors.shape
    block_len = length // block_count
    window_blocks = 3 * block_count
    full_gain, complete_query, complete_key, complete_value, complete_output = (
        lax.all_gather(norm_gain, "member", axis=0, tiled=True),
        lax.all_gather(w_query, "member", axis=0, tiled=True),
        lax.all_gather(w_key, "member", axis=0, tiled=True),
        lax.all_gather(w_value, "member", axis=0, tiled=True),
        lax.all_gather(w_out, "member", axis=0, tiled=True),
    )
    hidden_width = complete_query.shape[1]
    pair_width = 2 * HEAD_DIM
    pair_count = hidden_width // pair_width
    score_scale = HEAD_DIM ** (-0.5)
    inputs_float = inputs.astype(jnp.float32)
    inverse_rms = lax.rsqrt(jnp.mean(inputs_float * inputs_float, axis=-1, keepdims=True) + EPSILON)
    gain_float = full_gain.astype(jnp.float32)
    normalized_input = (inputs_float * inverse_rms * gain_float).astype(jnp.bfloat16)
    query = jnp.einsum(
        "fbi,iy->fby", normalized_input, complete_query, preferred_element_type=jnp.float32
    ).astype(jnp.bfloat16)
    key_rows = jnp.einsum(
        "fbi,iy->fby", normalized_input, complete_key, preferred_element_type=jnp.float32
    ).astype(jnp.bfloat16)
    value_rows = jnp.einsum(
        "fbi,iy->fby", normalized_input, complete_value, preferred_element_type=jnp.float32
    ).astype(jnp.bfloat16)
    key_value = jnp.concatenate([key_rows, value_rows], axis=-1)
    extended = extended_2(key_value, (("domain", 1),), length)
    domain_rank = lax.axis_index("domain")
    local_index = neighbors - (domain_rank - 1) * block_count
    present = slot_valid > 0
    window_ids = jnp.arange(window_blocks, dtype=jnp.int32)
    key_all = extended[..., :hidden_width]
    value_all = extended[..., hidden_width:]
    score_spec = "sbqgd,skgd->sbgqk"
    mix_spec = "sbgqk,skgd->sbqgd"
    back_spec = "sbgqk,sbqgd->skgd"
    matches = jnp.logical_and(
        local_index[:, :, None] == window_ids[None, None, :], present[:, :, None]
    )
    included = jnp.any(matches, axis=1)
    key_mask = jnp.repeat(included, block_len, axis=1)

    def pair_keys(pair_index):
        key_pair = pair_columns(key_all, pair_index, pair_width).reshape(
            samples, window_blocks * block_len, 2, HEAD_DIM
        )
        value_pair = pair_columns(value_all, pair_index, pair_width).reshape(
            samples, window_blocks * block_len, 2, HEAD_DIM
        )
        return (key_pair, value_pair)

    def to_window(grad_keys):
        return grad_keys.reshape(samples, window_blocks * block_len, pair_width)

    def pair_probability(pair_index):
        query_pair = pair_columns(query, pair_index, pair_width).reshape(
            samples, block_count, block_len, 2, HEAD_DIM
        )
        key_pair, value_pair = pair_keys(pair_index)
        scores = (
            jnp.einsum(score_spec, query_pair, key_pair, preferred_element_type=jnp.float32)
            * score_scale
        )
        scores = jnp.where(key_mask[None, :, None, None, :], scores, MASKED)
        row_max = jnp.max(scores, axis=-1, keepdims=True)
        shifted = jnp.exp(scores - row_max)
        probability = shifted / jnp.sum(shifted, axis=-1, keepdims=True)
        return (query_pair, key_pair, value_pair, probability)

    def forward_pair(pair_index):
        query_pair, key_pair, value_pair, probability = pair_probability(pair_index)
        prob_bf = probability.astype(jnp.bfloat16)
        mixed_pair = jnp.einsum(mix_spec, prob_bf, value_pair, preferred_element_type=jnp.float32)
        return mixed_pair.astype(jnp.bfloat16).reshape(samples, length, pair_width)

    attention_pairs = lax.map(forward_pair, jnp.arange(pair_count))
    neighbour_attention = jnp.transpose(attention_pairs, (1, 2, 0, 3)).reshape(
        samples, length, hidden_width
    )
    attn_out = jnp.einsum(
        "qny,yb->qnb", neighbour_attention, complete_output, preferred_element_type=jnp.float32
    ).astype(jnp.bfloat16)
    d_attention = jnp.einsum(
        "yjz,bz->yjb", output_cotangent, complete_output, preferred_element_type=jnp.float32
    ).astype(jnp.bfloat16)
    row_share = hidden_width // lax.axis_size("member")
    member_total = samples * lax.axis_size("member")
    incomplete_gradient = jnp.einsum(
        "rfe,rfu->eu", neighbour_attention, output_cotangent, preferred_element_type=jnp.float32
    )
    total_grad = lax.psum(incomplete_gradient, ("domain", "member"))
    grad_mine = lax.dynamic_slice_in_dim(
        total_grad, lax.axis_index("member") * row_share, row_share, 0
    )
    grad_wout = grad_mine / member_total

    def backward_pair(pair_index):
        query_pair, key_pair, value_pair, probability = pair_probability(pair_index)
        prob_bf = probability.astype(jnp.bfloat16)
        grad_pair = pair_columns(d_attention, pair_index, pair_width).reshape(
            samples, block_count, block_len, 2, HEAD_DIM
        )
        d_prob = jnp.einsum(score_spec, grad_pair, value_pair, preferred_element_type=jnp.float32)
        delta = jnp.sum(probability * d_prob, axis=-1, keepdims=True)
        d_score = (probability * (d_prob - delta) * score_scale).astype(jnp.bfloat16)
        d_query_pair = jnp.einsum(mix_spec, d_score, key_pair, preferred_element_type=jnp.float32)
        d_query_pair = d_query_pair.astype(jnp.bfloat16).reshape(samples, length, pair_width)
        d_key_pair = jnp.einsum(back_spec, d_score, query_pair, preferred_element_type=jnp.float32)
        d_value_pair = jnp.einsum(back_spec, prob_bf, grad_pair, preferred_element_type=jnp.float32)
        return (d_query_pair, to_window(d_key_pair), to_window(d_value_pair))

    query_grads, key_grads, value_grads = lax.map(backward_pair, jnp.arange(pair_count))
    query_cotangent = jnp.transpose(query_grads, (1, 2, 0, 3)).reshape(
        samples, length, hidden_width
    )
    key_ext = jnp.transpose(key_grads, (1, 2, 0, 3)).reshape(samples, 3 * length, hidden_width)
    value_ext = jnp.transpose(value_grads, (1, 2, 0, 3)).reshape(samples, 3 * length, hidden_width)
    ext_grad = jnp.concatenate([key_ext, value_ext], axis=-1)
    lower_rim = ext_grad[:, :length]
    own_part = ext_grad[:, length : 2 * length]
    upper_rim = ext_grad[:, 2 * length :]
    rims_half = jnp.concatenate([lower_rim, upper_rim], axis=1).astype(jnp.bfloat16)
    returned = extended_2(rims_half, (("domain", 1),), length)
    from_below = returned[:, :length].astype(jnp.float32)
    from_above = returned[:, 3 * length :].astype(jnp.float32)
    kv_total = own_part + from_below + from_above
    kv_grad = kv_total.astype(jnp.bfloat16)
    key_cotangent = kv_grad[..., :hidden_width]
    value_cotangent = kv_grad[..., hidden_width:]
    normed_cotangent = jnp.einsum(
        "qja,ga->qjg", query_cotangent, complete_query, preferred_element_type=jnp.float32
    )
    normed_cotangent = normed_cotangent + jnp.einsum(
        "qja,ga->qjg", key_cotangent, complete_key, preferred_element_type=jnp.float32
    )
    normed_cotangent = normed_cotangent + jnp.einsum(
        "qja,ga->qjg", value_cotangent, complete_value, preferred_element_type=jnp.float32
    )
    scaled_grad = normed_cotangent * gain_float
    inner_mean = jnp.mean(scaled_grad * inputs_float, axis=-1, keepdims=True)
    d_input = inverse_rms * scaled_grad - inputs_float * inverse_rms**3 * inner_mean
    return (attn_out, d_input.astype(jnp.bfloat16), grad_wout)


def solution(mesh):
    placed = (
        P("member", "domain", None),
        P("member"),
        P("member", None),
        P("member", None),
        P("member", None),
        P("member", None),
        P("domain", None),
        P("domain", None),
        P("member", "domain", None),
    )
    return jax.shard_map(
        shards,
        mesh=mesh,
        in_specs=placed,
        out_specs=(P("member", "domain", None), P("member", "domain", None), P("member", None)),
        check_vma=False,
    )
```

profile of v0, /device:TPU:1, one launch (start us, length us, event | category | flops | bytes accessed | tf_op | source)
XLA Modules:
  0.0 901.7 jit_solution(3319372591805515954)
XLA Ops:
  11.5 22.8 %all-gather = bf16[8,1,128]{2,1,0:T(2,128)(2,1)S(1)} all-gather(bf16[1,1,128]{2,1,0:T(2,128)(2,1)} %bitcast.205), channel_id=1, replica_groups=mesh['domain'=64,'member'=8] {'member'}, dimensions={0}, use_global_device_ids=true | all-gather | bytes 2304 | tf_op jit(solution)/shard_map/all_gather | solution.py:36
  35.0 28.1 %all-gather.8.cloned.1.call-done = bf16[1024,512]{1,0:T(8,128)(2,1)} async-done(((bf16[128,512]{1,0:T(8,128)(2,1)}), bf16[1024,512]{1,0:T(8,128)(2,1)}) %all-gather.8.cloned.1.call-update) | async-done | bytes 1048592 | tf_op jit(solution)/shard_map/all_gather | solution.py:39
  65.2 42.2 %all-gather.6.cloned.1.call-done = bf16[1024,512]{1,0:T(8,128)(2,1)} async-done(((bf16[128,512]{1,0:T(8,128)(2,1)}), bf16[1024,512]{1,0:T(8,128)(2,1)}) %all-gather.6.cloned.1.call-update) | async-done | bytes 1048592 | tf_op jit(solution)/shard_map/all_gather | solution.py:38
  111.5 4.9 collective-permute-start
  116.7 37.4 %all-gather.12.cloned.1.call-done = bf16[512,1024]{1,0:T(8,128)(2,1)} async-done(((bf16[64,1024]{1,0:T(8,128)(2,1)}), bf16[512,1024]{1,0:T(8,128)(2,1)}) %all-gather.12.cloned.1.call-update) | async-done | bytes 1048592 | tf_op jit(solution)/shard_map/all_gather | solution.py:40
  154.0 2.6 convolution_convert_fusion.2
  156.6 59.6 %all-gather.10.cloned.1.call-done = bf16[1024,512]{1,0:T(8,128)(2,1)} async-done(((bf16[128,512]{1,0:T(8,128)(2,1)}), bf16[1024,512]{1,0:T(8,128)(2,1)}) %all-gather.10.cloned.1.call-update) | async-done | bytes 1048592 | tf_op jit(solution)/shard_map/all_gather | solution.py:37
  216.2 2.6 convolution_convert_fusion.3
  224.2 34.7 %while.26 = (s32[]{:T(128)}, bf16[4,2,192,128]{3,2,1,0:T(8,128)(2,1)}, s32[4]{0:T(128)S(1)}, bf16[2,576,512]{1,2,0:T(8,128)(2,1)}, bf16[2,576,512]{1,2,0:T(8,128...) while((s32[]{:T(128)}, ...), condition=%wide.region_5.6_spmd.clone, body=%wide.region_2.5_spmd.clone.sunk | while | flops 117278592 | bytes 8469142 | solution.py:109
  259.7 121.8 %while.27 = (s32[]{:T(128)}, bf16[4,2,192,128]{3,2,1,0:T(8,128)(2,1)}, f32[4,2,576,128]{2,3,1,0:T(8,128)}, f32[4,2,576,128]{2,3,1,0:T(8,128)}, s32[4]{0:T(128)S(...) while((s32[]{:T(128)}, ...), condition=%wide.region_10.11_spmd.clone, body=%wide.region_6.0_spmd.clone.sunk | while | flops 293343744 | bytes 26301140 | solution.py:145
  269.1 7.8 fusion.143
  278.8 2.4 fusion.144
  281.2 7.7 fusion.145
  299.5 7.8 fusion.143
  309.2 2.4 fusion.144
  311.6 7.7 fusion.145
  329.9 7.8 fusion.143
  339.6 2.4 fusion.144
  342.0 7.7 fusion.145
  360.4 7.8 fusion.143
  370.1 2.4 fusion.144
  372.5 7.7 fusion.145
  381.4 3.2 copy.65
  386.8 3.5 constant_dynamic-update-slice_fusion.5
  390.2 2.6 copy.66
  392.8 2.7 reshape.82
  397.3 2.7 convert.6
  402.3 4.9 collective-permute-start.2
  409.3 2.8 convolution_convert_fusion.1
  412.7 9.3 %collective-permute-done.3 = bf16[2,192,1024]{2,1,0:T(8,128)(2,1)} collective-permute-done((bf16[2,192,1024]{2,1,0:T(8,128)(2,1)}, bf16[2,192,1024]{2,1,0:T(8,128)(2,1)}, u32[]{:S(2)}, u32[]{:S(2)}) %collective-permute-start.3) | collective-permute-done | bytes 786464 | tf_op jit(solution)/shard_map/ppermute | solution.py:19
  422.6 2.2 fusion.58
  428.5 465.0 %all-reduce.2.cloned.1.call-done = f32[512,1024]{1,0:T(8,128)} async-done(((f32[512,1024]{1,0:T(8,128)}), f32[512,1024]{1,0:T(8,128)}) %all-reduce.2.cloned.1.call-update) | async-done | bytes 2097168 | tf_op jit(solution)/shard_map/psum | solution.py:124
  (198 shorter events, 111.2 us)
Async XLA Ops:
  7.2 146.9 %copy-start = (bf16[2,192,1024]{2,1,0:T(8,128)(2,1)S(1)}, bf16[2,192,1024]{2,1,0:T(8,128)(2,1)}, u32[]{:S(2)}) copy-start(bf16[2,192,1024]{2,1,0:T(8,128)(2,1)} %param.21) | copy-start | bytes 2359300
  7.2 55.9 %all-gather.8.cloned.1.call-start = ((), (), s32[]{:S(2)}) async-start(), calls=%async_computation.1 | async-start | bytes 1179648 | tf_op jit(solution)/shard_map/all_gather | solution.py:39
  7.9 99.4 %all-gather.6.cloned.1.call-start = ((), (), s32[]{:S(2)}) async-start(), calls=%async_computation | async-start | bytes 1179648 | tf_op jit(solution)/shard_map/all_gather | solution.py:38
  8.7 145.4 %all-gather.12.cloned.1.call-start = ((), (), s32[]{:S(2)}) async-start(), calls=%async_computation.3 | async-start | bytes 1179648 | tf_op jit(solution)/shard_map/all_gather | solution.py:40
  9.4 206.8 %all-gather.10.cloned.1.call-start = ((), (), s32[]{:S(2)}) async-start(), calls=%async_computation.2 | async-start | bytes 1179648 | tf_op jit(solution)/shard_map/all_gather | solution.py:37
  10.0 97.4 %copy-start.2 = (bf16[2,192,1024]{2,1,0:T(8,128)(2,1)S(1)}, bf16[2,192,1024]{2,1,0:T(8,128)(2,1)}, u32[]{:S(2)}) copy-start(bf16[2,192,1024]{2,1,0:T(8,128)(2,1)} %param.13) | copy-start | bytes 2359300
  10.0 883.5 %all-reduce.2.cloned.1.call-start = ((), (), s32[]{:S(2)}) async-start(), calls=%async_computation.4 | async-start | bytes 4194304 | tf_op jit(solution)/shard_map/psum | solution.py:124
  65.1 51.2 %copy-start.10 = (s32[3,9]{1,0:T(4,128)S(1)}, s32[3,9]{1,0:T(4,128)}, u32[]{:S(2)}) copy-start(s32[3,9]{1,0:T(4,128)} %param.20) | copy-start | bytes 328
  110.2 108.6 %collective-permute-start.1 = (bf16[2,192,1024]{2,1,0:T(8,128)(2,1)}, bf16[2,192,1024]{2,1,0:T(8,128)(2,1)S(1)}, u32[]{:S(2)}, u32[]{:S(2)}) collective-permute-start(bf16[2,192,1024]{2,1,0:T(8,128)(2,1)} %pad_maximum_fusion.1), channel_id=1, source_target_pairs={{8,0},{16,8},{24,16},{32,24},{40,32},{48,40},{56,48},{64,56},{72,6... | collective-permute-start | bytes 2359304 | tf_op jit(solution)/shard_map/ppermute | solution.py:19
  111.5 107.3 %collective-permute-start = (bf16[2,192,1024]{2,1,0:T(8,128)(2,1)}, bf16[2,192,1024]{2,1,0:T(8,128)(2,1)}, u32[]{:S(2)}, u32[]{:S(2)}) collective-permute-start(bf16[2,192,1024]{2,1,0:T(8,128)(2,1)} %pad_maximum_fusion.1), channel_id=1, source_target_pairs={{0,8},{8,16},{16,24},{24,32},{32,40},{40,48},{48,56},{56,64},{64,7... | collective-permute-start | bytes 2359304 | tf_op jit(solution)/shard_map/ppermute | solution.py:18
  281.2 7.7 copy-start.1
  311.6 7.7 copy-start.1
  342.0 7.7 copy-start.1
  372.5 7.7 copy-start.1
  386.8 3.5 copy-start.4
  400.0 7.2 copy-start.5
  401.0 21.0 %collective-permute-start.3 = (bf16[2,192,1024]{2,1,0:T(8,128)(2,1)}, bf16[2,192,1024]{2,1,0:T(8,128)(2,1)}, u32[]{:S(2)}, u32[]{:S(2)}) collective-permute-start(bf16[2,192,1024]{2,1,0:T(8,128)(2,1)} %get-tuple-element.247), channel_id=1, source_target_pairs={{8,0},{16,8},{24,16},{32,24},{40,32},{48,40},{56,48},{64,56},{72,6... | collective-permute-start | bytes 2359304 | tf_op jit(solution)/shard_map/ppermute | solution.py:19
  402.3 20.3 %collective-permute-start.2 = (bf16[2,192,1024]{2,1,0:T(8,128)(2,1)S(1)}, bf16[2,192,1024]{2,1,0:T(8,128)(2,1)}, u32[]{:S(2)}, u32[]{:S(2)}) collective-permute-start(bf16[2,192,1024]{2,1,0:T(8,128)(2,1)S(1)} %get-tuple-element.246), channel_id=1, source_target_pairs={{0,8},{8,16},{16,24},{24,32},{32,40},{40,48},{48,56},{56,64},{64,7... | collective-permute-start | bytes 2359304 | tf_op jit(solution)/shard_map/ppermute | solution.py:18
  409.3 2.8 copy-start.6
  409.3 2.8 copy-start.8
  412.7 12.2 %copy-start.7 = (bf16[1024,512]{1,0:T(8,128)(2,1)S(1)}, bf16[1024,512]{1,0:T(8,128)(2,1)}, u32[]{:S(2)}) copy-start(bf16[1024,512]{1,0:T(8,128)(2,1)} %all-gather.6.cloned.1.call-done) | copy-start | bytes 3145732
  424.9 1.1 copy-start.3
  424.9 1.5 copy-start.9
Sparse Core Ops, SparseCore 0:
  10.1 52.8 all-gather.7
  65.2 42.0 all-gather.5
  109.5 44.4 all-gather.11
  156.0 60.1 all-gather.9
  409.4 484.0 all-reduce.1
where the time goes:
time: 903 us; the launch traced here: 902 us
  waiting for transfers between devices  645 us (71%)
  matrix products  106 us (12%)
  local copies, waits for them, and re-layouts  73.6 us (8%)
  blocking collectives  22.8 us (3%)
  other arithmetic  22.2 us (2%)
  between operations  14 us (2%)
  starting transfers between devices  12.5 us (1%)
    psum x1, waiting for transfers between devices, shards(): total_grad = lax.psum(incomplete_gradient, ('domain', 'member'))  465 us
    all_gather x1, waiting for transfers between devices, shards(): lax.all_gather(w_query, 'member', axis=0, tiled=True)  59.6 us
    all_gather x1, waiting for transfers between devices, shards(): lax.all_gather(w_key, 'member', axis=0, tiled=True)  42.2 us
    all_gather x1, waiting for transfers between devices, shards(): lax.all_gather(w_out, 'member', axis=0, tiled=True)  37.4 us
    dot_general x4, matrix products, backward_pair(): jnp.einsum(mix_spec, d_score, key_pair, preferred_element_type=jnp.float32)  31.3 us
    dot_general x4, matrix products, backward_pair(): jnp.einsum(back_spec, d_score, query_pair, preferred_element_type=jnp.flo...  30.7 us
    all_gather x1, waiting for transfers between devices, shards(): lax.all_gather(w_value, 'member', axis=0, tiled=True)  28.1 us
    dynamic_slice x24, local copies, waits for them, and re-layouts, pair_columns(): lax.dynamic_slice_in_dim(field, pair_index * pair_width, pair_width, fiel...  23.5 us
  transfers between devices with their start and end apart: 9, of which 7 were waited for; matrix products, arithmetic and copies ran while one was open for 3% of the time, Pallas kernels for 0%

commit v1 on v0

--- a/solution.py
+++ b/solution.py
@@ -1,3 +1,4 @@
+import functools
 import jax
 import jax.numpy as jnp
 from jax import lax
@@ -6,6 +7,14 @@
 HEAD_DIM = 64
 EPSILON = 1e-06
 MASKED = -1e30
+
+
+def derive_roots(sheet, comm_axis, across):
+    back = lax.psum(sheet, axis_name=comm_axis)
+    return lax.psum(back, axis_name=across)
+
+
+ranges_draft = functools.partial(derive_roots, comm_axis="domain", across="member")
 
 
 def extended_2(value, sides, width):
@@ -121,7 +130,7 @@
     incomplete_gradient = jnp.einsum(
         "rfe,rfu->eu", neighbour_attention, output_cotangent, preferred_element_type=jnp.float32
     )
-    total_grad = lax.psum(incomplete_gradient, ("domain", "member"))
+    total_grad = ranges_draft(incomplete_gradient)
     grad_mine = lax.dynamic_slice_in_dim(
         total_grad, lax.axis_index("member") * row_share, row_share, 0
     )

time: 903 us -> 1140 us (1.26)
  waiting for transfers between devices: 645 us -> 890 us
    psum x1 -> x2, waiting for transfers between devices: 465 us -> 721 us  [the longest x1 546 us: derive_roots(): back = lax.psum(sheet, axis_name=comm_axis)]
  transfers between devices with their start and end apart: 9 -> 10, of which waited for: 7 -> 6; matrix products, arithmetic and copies ran while one was open for 3% -> 13% of each run, Pallas kernels for 0% -> 0%
where the time goes in v1:
time: 1140 us
  waiting for transfers between devices  890 us (78%)
  matrix products  106 us (9%)
  local copies, waits for them, and re-layouts  68.9 us (6%)
  blocking collectives  22.8 us (2%)
  other arithmetic  20.4 us (2%)
  between operations  14.3 us (1%)
  starting transfers between devices  12.8 us (1%)
    psum x1, waiting for transfers between devices, derive_roots(): back = lax.psum(sheet, axis_name=comm_axis)  546 us
    psum x1, waiting for transfers between devices, derive_roots(): return lax.psum(back, axis_name=across)  174 us
    all_gather x1, waiting for transfers between devices, shards(): lax.all_gather(w_query, 'member', axis=0, tiled=True)  59.6 us
    all_gather x1, waiting for transfers between devices, shards(): lax.all_gather(w_key, 'member', axis=0, tiled=True)  42.2 us
    all_gather x1, waiting for transfers between devices, shards(): lax.all_gather(w_out, 'member', axis=0, tiled=True)  37.3 us
    dot_general x4, matrix products, backward_pair(): jnp.einsum(back_spec, d_score, query_pair, preferred_element_type=jnp.flo...  31.2 us
    dot_general x4, matrix products, backward_pair(): jnp.einsum(mix_spec, d_score, key_pair, preferred_element_type=jnp.float32)  29.6 us
    all_gather x1, waiting for transfers between devices, shards(): lax.all_gather(w_value, 'member', axis=0, tiled=True)  28.1 us
  transfers between devices with their start and end apart: 10, of which 6 were waited for; matrix products, arithmetic and copies ran while one was open for 13% of the time, Pallas kernels for 0%

profile of v1, /device:TPU:1, one launch (start us, length us, event | category | flops | bytes accessed | tf_op | source)
XLA Modules:
  0.0 1141.4 jit_solution(14979146941698480643)
XLA Ops:
  11.5 22.8 %all-gather = bf16[8,1,128]{2,1,0:T(2,128)(2,1)S(1)} all-gather(bf16[1,1,128]{2,1,0:T(2,128)(2,1)} %bitcast.205), channel_id=1, replica_groups=mesh['domain'=64,'member'=8] {'member'}, dimensions={0}, use_global_device_ids=true | all-gather | bytes 2304 | tf_op jit(solution)/shard_map/all_gather | solution.py:45
  35.0 28.1 %all-gather.8.cloned.1.call-done = bf16[1024,512]{1,0:T(8,128)(2,1)} async-done(((bf16[128,512]{1,0:T(8,128)(2,1)}), bf16[1024,512]{1,0:T(8,128)(2,1)}) %all-gather.8.cloned.1.call-update) | async-done | bytes 1048592 | tf_op jit(solution)/shard_map/all_gather | solution.py:48
  65.2 42.2 %all-gather.6.cloned.1.call-done = bf16[1024,512]{1,0:T(8,128)(2,1)} async-done(((bf16[128,512]{1,0:T(8,128)(2,1)}), bf16[1024,512]{1,0:T(8,128)(2,1)}) %all-gather.6.cloned.1.call-update) | async-done | bytes 1048592 | tf_op jit(solution)/shard_map/all_gather | solution.py:47
  111.5 4.9 collective-permute-start
  116.7 37.3 %all-gather.12.cloned.1.call-done = bf16[512,1024]{1,0:T(8,128)(2,1)} async-done(((bf16[64,1024]{1,0:T(8,128)(2,1)}), bf16[512,1024]{1,0:T(8,128)(2,1)}) %all-gather.12.cloned.1.call-update) | async-done | bytes 1048592 | tf_op jit(solution)/shard_map/all_gather | solution.py:49
  154.0 2.6 convolution_convert_fusion.2
  156.6 59.6 %all-gather.10.cloned.1.call-done = bf16[1024,512]{1,0:T(8,128)(2,1)} async-done(((bf16[128,512]{1,0:T(8,128)(2,1)}), bf16[1024,512]{1,0:T(8,128)(2,1)}) %all-gather.10.cloned.1.call-update) | async-done | bytes 1048592 | tf_op jit(solution)/shard_map/all_gather | solution.py:46
  216.2 2.6 convolution_convert_fusion.3
  224.1 34.7 %while.26 = (s32[]{:T(128)}, bf16[4,2,192,128]{3,2,1,0:T(8,128)(2,1)}, s32[4]{0:T(128)S(1)}, bf16[2,576,512]{1,2,0:T(8,128)(2,1)}, bf16[2,576,512]{1,2,0:T(8,128...) while((s32[]{:T(128)}, ...), condition=%wide.region_5.6_spmd.clone, body=%wide.region_2.5_spmd.clone.sunk | while | flops 117278592 | bytes 8469142 | solution.py:118
  258.8 3.0 convolution_bitcast_fusion
  262.1 115.1 %while.27 = (s32[]{:T(128)}, bf16[4,2,192,128]{3,2,1,0:T(8,128)(2,1)S(1)}, f32[4,2,576,128]{2,3,1,0:T(8,128)}, f32[4,2,576,128]{2,3,1,0:T(8,128)}, s32[4]{0:T(12...) while((s32[]{:T(128)}, ...), condition=%wide.region_10.11_spmd.clone, body=%wide.region_6.0_spmd.clone.sunk | while | flops 293343744 | bytes 26301140 | solution.py:154
  271.8 7.4 fusion.143
  279.5 2.4 fusion.144
  281.9 7.8 fusion.145
  300.6 7.4 fusion.143
  308.3 2.4 fusion.144
  310.7 7.8 fusion.145
  329.3 7.4 fusion.143
  337.0 2.4 fusion.144
  339.4 7.8 fusion.145
  358.1 7.4 fusion.143
  365.8 2.4 fusion.144
  368.2 7.8 fusion.145
  377.2 4.1 copy.65
  381.3 2.7 reshape.81
  384.0 4.1 copy.66
  388.1 3.6 reshape.82
  398.1 4.9 collective-permute-start.2
  403.0 546.2 %all-reduce.3.cloned.1.call-done = f32[512,1024]{1,0:T(8,128)} async-done(((f32[512,1024]{1,0:T(8,128)}), f32[512,1024]{1,0:T(8,128)}) %all-reduce.3.cloned.1.call-update) | async-done | bytes 2097168 | tf_op jit(solution)/shard_map/psum | solution.py:13
  949.3 2.8 convolution_convert_fusion.1
  952.7 2.3 fusion.58
  958.5 174.4 %all-reduce.5.cloned.1.call-done = f32[512,1024]{1,0:T(8,128)} async-done(((f32[512,1024]{1,0:T(8,128)}), f32[512,1024]{1,0:T(8,128)}) %all-reduce.5.cloned.1.call-update) | async-done | bytes 2097168 | tf_op jit(solution)/shard_map/psum | solution.py:14
  (203 shorter events, 102.7 us)
Async XLA Ops:
  7.2 146.9 %copy-start = (bf16[2,192,1024]{2,1,0:T(8,128)(2,1)S(1)}, bf16[2,192,1024]{2,1,0:T(8,128)(2,1)}, u32[]{:S(2)}) copy-start(bf16[2,192,1024]{2,1,0:T(8,128)(2,1)} %param.21) | copy-start | bytes 2359300
  7.2 55.9 %all-gather.8.cloned.1.call-start = ((), (), s32[]{:S(2)}) async-start(), calls=%async_computation.1 | async-start | bytes 1179648 | tf_op jit(solution)/shard_map/all_gather | solution.py:48
  7.9 99.4 %all-gather.6.cloned.1.call-start = ((), (), s32[]{:S(2)}) async-start(), calls=%async_computation | async-start | bytes 1179648 | tf_op jit(solution)/shard_map/all_gather | solution.py:47
  8.7 145.4 %all-gather.12.cloned.1.call-start = ((), (), s32[]{:S(2)}) async-start(), calls=%async_computation.3 | async-start | bytes 1179648 | tf_op jit(solution)/shard_map/all_gather | solution.py:49
  9.4 206.8 %all-gather.10.cloned.1.call-start = ((), (), s32[]{:S(2)}) async-start(), calls=%async_computation.2 | async-start | bytes 1179648 | tf_op jit(solution)/shard_map/all_gather | solution.py:46
  10.0 97.4 %copy-start.5 = (bf16[2,192,1024]{2,1,0:T(8,128)(2,1)S(1)}, bf16[2,192,1024]{2,1,0:T(8,128)(2,1)}, u32[]{:S(2)}) copy-start(bf16[2,192,1024]{2,1,0:T(8,128)(2,1)} %param.13) | copy-start | bytes 2359300
  10.0 939.2 %all-reduce.3.cloned.1.call-start = ((), (), s32[]{:S(2)}) async-start(), calls=%async_computation.4 | async-start | bytes 4194304 | tf_op jit(solution)/shard_map/psum | solution.py:13
  65.1 51.3 %copy-start.11 = (s32[3,9]{1,0:T(4,128)S(1)}, s32[3,9]{1,0:T(4,128)}, u32[]{:S(2)}) copy-start(s32[3,9]{1,0:T(4,128)} %param.20) | copy-start | bytes 328
  110.2 108.6 %collective-permute-start.1 = (bf16[2,192,1024]{2,1,0:T(8,128)(2,1)}, bf16[2,192,1024]{2,1,0:T(8,128)(2,1)S(1)}, u32[]{:S(2)}, u32[]{:S(2)}) collective-permute-start(bf16[2,192,1024]{2,1,0:T(8,128)(2,1)} %pad_maximum_fusion.1), channel_id=1, source_target_pairs={{8,0},{16,8},{24,16},{32,24},{40,32},{48,40},{56,48},{64,56},{72,6... | collective-permute-start | bytes 2359304 | tf_op jit(solution)/shard_map/ppermute | solution.py:28
  111.5 107.3 %collective-permute-start = (bf16[2,192,1024]{2,1,0:T(8,128)(2,1)}, bf16[2,192,1024]{2,1,0:T(8,128)(2,1)}, u32[]{:S(2)}, u32[]{:S(2)}) collective-permute-start(bf16[2,192,1024]{2,1,0:T(8,128)(2,1)} %pad_maximum_fusion.1), channel_id=1, source_target_pairs={{0,8},{8,16},{16,24},{24,32},{32,40},{40,48},{48,56},{56,64},{64,7... | collective-permute-start | bytes 2359304 | tf_op jit(solution)/shard_map/ppermute | solution.py:27
  261.8 871.1 %all-reduce.5.cloned.1.call-start = ((), (), s32[]{:S(2)}) async-start(), calls=%async_computation.5 | async-start | bytes 4194304 | tf_op jit(solution)/shard_map/psum | solution.py:14
  281.9 7.8 copy-start.2
  310.7 7.8 copy-start.2
  339.4 7.8 copy-start.2
  368.2 7.8 copy-start.2
  391.7 1.7 copy-start.4
  393.7 2.1 copy-start.3
  395.8 553.5 %copy-start.7 = (bf16[4,2,192,128]{3,2,1,0:T(8,128)(2,1)S(1)}, bf16[4,2,192,128]{3,2,1,0:T(8,128)(2,1)}, u32[]{:S(2)}) copy-start(bf16[4,2,192,128]{3,2,1,0:T(8,128)(2,1)} %get-tuple-element.94) | copy-start | bytes 1179652
  396.8 555.8 %collective-permute-start.3 = (bf16[2,192,1024]{2,1,0:T(8,128)(2,1)}, bf16[2,192,1024]{2,1,0:T(8,128)(2,1)}, u32[]{:S(2)}, u32[]{:S(2)}) collective-permute-start(bf16[2,192,1024]{2,1,0:T(8,128)(2,1)} %get-tuple-element.247), channel_id=1, source_target_pairs={{8,0},{16,8},{24,16},{32,24},{40,32},{48,40},{56,48},{64,56},{72,6... | collective-permute-start | bytes 2359304 | tf_op jit(solution)/shard_map/ppermute | solution.py:28
  398.1 554.5 %collective-permute-start.2 = (bf16[2,192,1024]{2,1,0:T(8,128)(2,1)S(1)}, bf16[2,192,1024]{2,1,0:T(8,128)(2,1)}, u32[]{:S(2)}, u32[]{:S(2)}) collective-permute-start(bf16[2,192,1024]{2,1,0:T(8,128)(2,1)S(1)} %get-tuple-element.246), channel_id=1, source_target_pairs={{0,8},{8,16},{16,24},{24,32},{32,40},{40,48},{48,56},{56,64},{64,7... | collective-permute-start | bytes 2359304 | tf_op jit(solution)/shard_map/ppermute | solution.py:27
  949.2 2.8 copy-start.9
  952.6 2.3 copy-start.8
  955.0 1.1 copy-start.6
  955.0 1.5 copy-start.10
  956.4 178.2 %copy-start.1 = (bf16[2,192,1024]{2,1,0:T(8,128)(2,1)S(1)}, bf16[2,192,1024]{2,1,0:T(8,128)(2,1)}, u32[]{:S(2)}) copy-start(bf16[2,192,1024]{2,1,0:T(8,128)(2,1)} %param.21) | copy-start | bytes 2359300
Sparse Core Ops, SparseCore 0:
  10.1 52.8 all-gather.7
  65.2 42.0 all-gather.5
  109.5 44.4 all-gather.11
  156.0 60.1 all-gather.9
  262.0 687.2 all-reduce.2
  952.0 180.8 all-reduce.4
